TPU v7x, 32 devices: a whole 2x2x4 slice. The times are simulated.
32 devices in a mesh: row: 4 (over x, core), col: 8 (over z, y).
Axes of the slice: x: 2, y: 2, z: 4, core: 2. Of those that a mesh axis runs over, the one named last changes fastest.
Arguments:
- tile_list: int32 [512, 2], P(('row', 'col')), may hold values from -1 to 63, as said below
- tile_values: bfloat16 [512, 512, 512], P(('row', 'col'))
- block_order: int32 [64], replicated, may hold values from 0 to 63, as said below
- basis: bfloat16 [64, 512, 256], P(('row', 'col')), may hold values from -8 to 8
Outputs:
- basis_out: bfloat16 [64, 512, 256], P(('row', 'col'))
- projected: float32 [256, 256], replicated
Inputs may be any that keep to these rules, and one draw needn't show every extreme that they name: `block_order`: A permutation of the channel blocks; slot p lies on device p // 2 in row-major order of (row, col). `tile_list`: slots of device (i, j) hold tiles whose row block sits in a slot of a device of row index i and whose column block sits in a slot of a device of column index j; each unordered pair of blocks appears at most once in all; empty slots hold -1 in both columns and may stand anywhere among a device's slots; every device holds at most 16 tiles and some device holds exactly 16.
All inputs are finite; a program needn't handle non-finite values.
Results may differ from a plain program's by a relative error of at most 0.0017.
Values may be sent and summed in bfloat16 or wider, within the bound.
A program may use at most 128 MiB of HBM per device.

v0:
```python
import jax
import jax.numpy as jnp
from jax import lax
from jax.sharding import PartitionSpec as P


def per_device(tile_list, tile_values, block_order, basis):
    rows_count = lax.axis_size("row")
    cols_count = lax.axis_size("col")
    own_blocks = basis.shape[0]
    edge = basis.shape[1]
    rank = basis.shape[2]
    blocks_all = block_order.shape[0]
    scale = jnp.sqrt(jnp.float32(blocks_all * edge))
    row_here = lax.axis_index("row")
    row_group = own_blocks * cols_count
    col_group = own_blocks * rows_count
    present = tile_list[:, 0] >= 0
    slot_range = jnp.arange(blocks_all, dtype=jnp.int32)
    ids_both = jnp.where(present[:, None], tile_list, 0)
    match = block_order[None, None, :] == ids_both[:, :, None]
    slots_both = jnp.sum(jnp.where(match, slot_range[None, None, :], 0), axis=2)
    first_slot = slots_both[:, 0]
    second_slot = slots_both[:, 1]
    row_local = jnp.where(present, first_slot - row_here * row_group, row_group)
    owner_second = second_slot // own_blocks
    col_local = jnp.where(
        present, owner_second // cols_count * own_blocks + second_slot % own_blocks, col_group
    )
    column_side = lax.all_gather(basis, "row", axis=0, tiled=True)
    row_side = lax.all_gather(basis, "col", axis=0, tiled=True)
    empty_block = jnp.zeros((1, edge, rank), basis.dtype)
    column_padded = jnp.concatenate([column_side, empty_block], axis=0)
    row_padded = jnp.concatenate([row_side, empty_block], axis=0)
    picked_col = column_padded[col_local]
    picked_row = row_padded[row_local]
    near_prod = jnp.einsum(
        "tab,tbk->tak", tile_values, picked_col, preferred_element_type=jnp.float32
    )
    far_prod = jnp.einsum(
        "tba,tbk->tak", tile_values, picked_row, preferred_element_type=jnp.float32
    )
    col_partial = (
        jnp.zeros((col_group, edge, rank), jnp.float32).at[col_local].add(far_prod, mode="drop")
    )
    row_partial = (
        jnp.zeros((row_group, edge, rank), jnp.float32).at[row_local].add(near_prod, mode="drop")
    )
    row_owned = lax.psum_scatter(row_partial, "col", scatter_dimension=0, tiled=True)
    upper_part = lax.optimization_barrier(col_partial.astype(jnp.bfloat16))
    remainder = col_partial - upper_part.astype(jnp.float32)
    middle_part = lax.optimization_barrier(remainder.astype(jnp.bfloat16))
    lower_part = (remainder - middle_part.astype(jnp.float32)).astype(jnp.bfloat16)
    pieces = jnp.concatenate([upper_part, middle_part, lower_part], axis=2)
    folded = jnp.einsum("sak,saj->kj", column_side, pieces, preferred_element_type=jnp.float32)
    tile_form = folded[:, :rank] + folded[:, rank : 2 * rank] + folded[:, 2 * rank :]
    projected = lax.psum((tile_form + tile_form.T) / scale, ("row", "col"))
    col_owned = lax.psum_scatter(col_partial, "row", scatter_dimension=0, tiled=True)
    product = (row_owned + col_owned).reshape(own_blocks * edge, rank)
    gram_term = jnp.dot(product.T, product, precision=lax.Precision.HIGHEST)
    gram = lax.psum(gram_term, ("row", "col"))
    first_factor = jnp.linalg.cholesky(gram)
    first_basis = lax.linalg.triangular_solve(
        first_factor, product, left_side=False, lower=True, transpose_a=True
    )
    second_term = jnp.dot(first_basis.T, first_basis, precision=lax.Precision.HIGHEST)
    second = lax.psum(second_term, ("row", "col"))
    second_factor = jnp.linalg.cholesky(second)
    final = lax.linalg.triangular_solve(
        second_factor, first_basis, left_side=False, lower=True, transpose_a=True
    )
    basis_out = (final * scale).astype(jnp.bfloat16).reshape(own_blocks, edge, rank)
    return (basis_out, projected)


def solution(mesh):
    in_specs = (
        P(("row", "col"), None),
        P(("row", "col"), None, None),
        P(),
        P(("row", "col"), None, None),
    )
    out_specs = (P(("row", "col"), None, None), P())
    return jax.shard_map(
        per_device, mesh=mesh, in_specs=in_specs, out_specs=out_specs, check_vma=False
    )
```

profile of v0, /device:TPU:0, one launch (start us, length us, event | category | flops | bytes accessed | tf_op | source)
XLA Modules:
  0.0 729.1 jit_solution(8188007919640402378)
XLA Ops:
  7.2 0.7 all-gather.5.cloned.1.call-update
  7.9 0.7 all-gather.3.cloned.1.call-update
  8.7 0.7 fusion.44
  9.4 0.7 broadcast_select_fusion
  10.1 0.8 select_reduce_fusion.2
  10.9 0.7 fusion.40
  11.6 74.0 %all-gather.5.cloned.1.call-done = bf16[16,512,256]{2,1,0:T(8,128)(2,1)} async-done(((bf16[2,512,256]{2,1,0:T(8,128)(2,1)}), bf16[16,512,256]{2,1,0:T(8,128)(2,1)}) %all-gather.5.cloned.1.call-update) | async-done | bytes 4194320 | tf_op jit(solution)/shard_map/all_gather | solution.py:31
  85.6 4.6 concatenate.13
  90.3 5.2 gather_fusion.1
  95.5 10.3 %convolution_bitcast_fusion = f32[16,512,256]{1,2,0:T(8,128)} fusion(bf16[16,512,256]{2,1,0:T(8,128)(2,1)} %gather_fusion.1, bf16[16,512,512]{2,1,0:T(8,128)(2,1)} %param.8), kind=kOutput, calls=%fused_computation.16 | convolution fusion | flops 2147483648 | bytes 20971520 | tf_op jit(solution)/shard_map/tba,tbk->tak/dot_general | solution.py:40
  105.8 9.3 %copy.39 = f32[16,512,256]{2,1,0:T(8,128)} copy(f32[16,512,256]{1,2,0:T(8,128)} %convolution_bitcast_fusion) | data formatting | bytes 16777216 | tf_op jit(solution)/shard_map/tba,tbk->tak/dot_general | solution.py:40
  115.1 2.3 broadcast_in_dim.54
  117.4 15.6 %scatter_fusion.1 = f32[8,512,256]{2,1,0:T(8,128)} fusion(f32[8,512,256]{2,1,0:T(8,128)} %broadcast_in_dim.54, s32[16]{0:T(128)S(1)} %get-tuple-element.46, f32[16,512,256]{2,1,0:T(8,128)} %copy.39), kind=kCustom, calls=%fused_computation.3 | custom fusion | flops 2097152 | bytes 25165888 | tf_op jit(solution)/shard_map/scatter-add | solution.py:44
  133.1 1.7 concatenate.12
  134.9 2.7 gather_fusion
  137.6 12.1 %convolution_bitcast_fusion.1 = f32[16,512,256]{1,2,0:T(8,128)} fusion(bf16[16,512,256]{2,1,0:T(8,128)(2,1)} %gather_fusion, bf16[16,512,512]{2,1,0:T(8,128)(2,1)} %param.8), kind=kOutput, calls=%fused_computation.17 | convolution fusion | flops 2147483648 | bytes 20971520 | tf_op jit(solution)/shard_map/tab,tbk->tak/dot_general | solution.py:37
  149.7 9.3 %copy.37 = f32[16,512,256]{2,1,0:T(8,128)} copy(f32[16,512,256]{1,2,0:T(8,128)} %convolution_bitcast_fusion.1) | data formatting | bytes 16777216 | tf_op jit(solution)/shard_map/tab,tbk->tak/dot_general | solution.py:37
  159.1 4.1 broadcast_in_dim.47
  163.1 15.9 %scatter_fusion = f32[16,512,256]{2,1,0:T(8,128)} fusion(f32[16,512,256]{2,1,0:T(8,128)} %broadcast_in_dim.47, s32[16]{0:T(128)S(1)} %fusion.37, f32[16,512,256]{2,1,0:T(8,128)} %copy.37), kind=kCustom, calls=%fused_computation.2 | custom fusion | flops 2097152 | bytes 25165888 | tf_op jit(solution)/shard_map/scatter-add | solution.py:47
  179.0 12.8 %all-reduce.7.cloned.1.call-start = ((), (), s32[]{:S(2)}) async-start(), calls=%async_computation.6 | async-start | bytes 524288 | tf_op jit(solution)/shard_map/psum | solution.py:61
  191.9 5.4 copy.46
  197.2 2.6 convert_element_type.19
  199.8 0.9 copy-done
  200.7 0.8 fusion.6
  201.5 1.0 subtract_convert_fusion
  202.5 0.6 copy-done.1
  203.1 1.8 fusion.7
  205.1 124.2 %reduce-scatter.3.cloned.1.call-done = f32[2,512,256]{2,1,0:T(8,128)} async-done(((f32[16,512,256]{2,1,0:T(8,128)}), f32[2,512,256]{2,1,0:T(8,128)}) %reduce-scatter.3.cloned.1.call-update) | async-done | bytes 1048592 | tf_op jit(solution)/shard_map/reduce_scatter | solution.py:49
  329.3 1.7 add.88
  331.0 2.5 convolution_bitcast_fusion.2
  333.6 0.8 fusion.17
  334.3 126.6 %all-reduce.7.cloned.1.call-done = f32[256,256]{0,1:T(8,128)} async-done(((f32[256,256]{0,1:T(8,128)}), f32[256,256]{0,1:T(8,128)}) %all-reduce.7.cloned.1.call-update) | async-done | bytes 262160 | tf_op jit(solution)/shard_map/psum | solution.py:61
  461.0 1.1 copy.42
  462.1 1.0 fusion.19
  463.1 11.7 %cholesky.130 = f32[128,128]{1,0:T(8,128)S(1)} custom-call(f32[128,128]{1,0:T(8,128)S(1)} %cholesky.194), custom_call_target="Cholesky" | custom-call | tf_op jit(solution)/shard_map/jit(cholesky)/cholesky | solution.py:62
  474.9 9.8 %custom-call.13 = f32[1,128,128]{1,2,0:T(8,128)S(1)} custom-call(f32[1,128,128]{2,1,0:T(8,128)S(1)} %get-tuple-element.59), custom_call_target="InvertDiagBlocksLowerTriangular" | custom-call | tf_op jit(solution)/shard_map/jit(cholesky)/cholesky | solution.py:62
  485.1 11.7 %cholesky.147 = f32[128,128]{1,0:T(8,128)S(1)} custom-call(f32[128,128]{1,0:T(8,128)S(1)} %convolution_subtract_fusion.3), custom_call_target="Cholesky" | custom-call | tf_op jit(solution)/shard_map/jit(cholesky)/cholesky | solution.py:62
  496.9 0.7 compare_reduce_fusion.2
  499.1 4.1 while.4
  499.1 0.6 fusion.65
  499.7 1.4 bitcast_dynamic-update-slice_fusion.4
  501.8 1.4 bitcast_dynamic-update-slice_fusion.4
  503.2 20.0 %custom-call.14 = f32[2,128,128]{1,2,0:T(8,128)S(1)} custom-call(f32[2,128,128]{2,1,0:T(8,128)S(1)} %get-tuple-element.18), custom_call_target="InvertDiagBlocksLowerTriangular" | custom-call | tf_op jit(solution)/shard_map/triangular_solve/custom-call.0 | solution.py:63
  523.2 0.6 fusion.15
  523.8 1.0 convolution_subtract_fusion.1
  524.8 0.6 fusion.25
  525.5 1.7 fusion.10
  527.2 128.6 %all-reduce.9.cloned.1.call-done = (f32[256,256]{0,1:T(8,128)}, f32[256,256]{0,1:T(8,128)}) async-done(((f32[256,256]{0,1:T(8,128)}, f32[256,256]{0,1:T(8,128)}), (f32[256,256]{0,1:T(8,128)}, f32[256,256]{0,1:T(8,128)})) %all-reduce.9.cloned.1.call-update) | async-done | bytes 524304 | tf_op jit(solution)/shard_map/psum | solution.py:67
  655.8 1.1 copy.44
  656.9 1.0 fusion.18
  657.9 11.7 %cholesky.164 = f32[128,128]{1,0:T(8,128)S(1)} custom-call(f32[128,128]{1,0:T(8,128)S(1)} %cholesky.197), custom_call_target="Cholesky" | custom-call | tf_op jit(solution)/shard_map/jit(cholesky)/cholesky | solution.py:68
  669.6 9.8 %custom-call.15 = f32[1,128,128]{1,2,0:T(8,128)S(1)} custom-call(f32[1,128,128]{2,1,0:T(8,128)S(1)} %get-tuple-element.55), custom_call_target="InvertDiagBlocksLowerTriangular" | custom-call | tf_op jit(solution)/shard_map/jit(cholesky)/cholesky | solution.py:68
  679.9 11.9 %cholesky.181 = f32[128,128]{1,0:T(8,128)S(1)} custom-call(f32[128,128]{1,0:T(8,128)S(1)} %convolution_subtract_fusion.2), custom_call_target="Cholesky" | custom-call | tf_op jit(solution)/shard_map/jit(cholesky)/cholesky | solution.py:68
  691.9 0.6 compare_reduce_fusion.1
  692.5 0.6 compare_reduce_fusion
  694.5 4.0 while.5
  695.1 1.4 bitcast_dynamic-update-slice_fusion.5
  697.1 1.4 bitcast_dynamic-update-slice_fusion.5
  698.5 19.7 %custom-call.16 = f32[2,128,128]{1,2,0:T(8,128)S(1)} custom-call(f32[2,128,128]{2,1,0:T(8,128)S(1)} %get-tuple-element.19), custom_call_target="InvertDiagBlocksLowerTriangular" | custom-call | tf_op jit(solution)/shard_map/triangular_solve/custom-call.0 | solution.py:69
  718.2 0.6 fusion.22
  718.9 0.6 convolution_subtract_fusion
  719.5 0.6 fusion.20
  720.2 1.0 copy.58
  721.2 0.8 copy.50
  (47 shorter events, 3.7 us)
Async XLA Ops:
  7.2 78.5 %all-gather.5.cloned.1.call-start = ((), (), s32[]{:S(2)}) async-start(), calls=%async_computation.4 | async-start | bytes 4718592 | tf_op jit(solution)/shard_map/all_gather | solution.py:31
  7.9 125.2 %all-gather.3.cloned.1.call-start = ((), (), s32[]{:S(2)}) async-start(), calls=%async_computation.2 | async-start | bytes 2621440 | tf_op jit(solution)/shard_map/all_gather | solution.py:30
  8.6 196.5 %reduce-scatter.5.cloned.1.call-start = ((), (), s32[]{:S(2)}) async-start(), calls=%async_computation.5 | async-start | bytes 5242880 | tf_op jit(solution)/shard_map/reduce_scatter | solution.py:58
  133.0 196.3 %reduce-scatter.3.cloned.1.call-start = ((), (), s32[]{:S(2)}) async-start(), calls=%async_computation.3 | async-start | bytes 9437184 | tf_op jit(solution)/shard_map/reduce_scatter | solution.py:49
  179.0 282.0 %all-reduce.7.cloned.1.call-start = ((), (), s32[]{:S(2)}) async-start(), calls=%async_computation.6 | async-start | bytes 524288 | tf_op jit(solution)/shard_map/psum | solution.py:61
  197.2 3.5 copy-start
  201.5 1.6 copy-start.1
  333.5 322.3 %all-reduce.9.cloned.1.call-start = ((), (), s32[]{:S(2)}) async-start(), calls=%async_computation.7 | async-start | bytes 1048576 | tf_op jit(solution)/shard_map/psum | solution.py:67
  679.7 41.5 %copy-start.2 = (f32[256,256]{0,1:T(8,128)S(1)}, f32[256,256]{0,1:T(8,128)}, u32[]{:S(2)}) copy-start(f32[256,256]{0,1:T(8,128)} %get-tuple-element.43) | copy-start | bytes 786436
Sparse Core Ops, SparseCore 0:
  10.1 75.5 all-gather.4
  87.2 21.0 all-gather.2
  133.1 45.1 reduce-scatter.4
  181.8 147.4 reduce-scatter.2
  335.2 125.7 all-reduce.6
  527.3 128.3 all-reduce.8
where the time goes:
time: 737 us; the launch traced here: 729 us
  waiting for transfers between devices  455 us (62%)
  other arithmetic  152 us (21%)
  local copies, waits for them, and re-layouts  58.5 us (8%)
  matrix products  33.5 us (5%)
  between operations  17.3 us (2%)
  starting transfers between devices  13 us (2%)
    psum x1, waiting for transfers between devices, per_device(): second = lax.psum(second_term, ('row', 'col'))  129 us
    psum x1, waiting for transfers between devices, per_device(): gram = lax.psum(gram_term, ('row', 'col'))  127 us
    reduce_scatter x1, waiting for transfers between devices, per_device(): lax.psum_scatter(row_partial, 'col', scatter_dimension=0, tiled=True)  124 us
    all_gather x1, waiting for transfers between devices, per_device(): row_side = lax.all_gather(basis, 'col', axis=0, tiled=True)  74 us
    another operation x7, other arithmetic, per_device(): second_factor = jnp.linalg.cholesky(second)  34.8 us
    another operation x6, other arithmetic, per_device(): first_factor = jnp.linalg.cholesky(gram)  34 us
    another operation x3, other arithmetic, per_device(): lax.linalg.triangular_solve(first_factor, product, left_side=False, lower...  20 us
    another operation x2, other arithmetic, per_device(): lax.linalg.triangular_solve(second_factor, first_basis, left_side=False,...  19.7 us
  transfers between devices with their start and end apart: 6, of which 4 were waited for; matrix products, arithmetic and copies ran while one was open for 15% of the time, Pallas kernels for 0%

commit v1 on v0

--- a/solution.py
+++ b/solution.py
@@ -2,6 +2,23 @@
 import jax.numpy as jnp
 from jax import lax
 from jax.sharding import PartitionSpec as P
+
+
+def laid_out(blocks, dim):
+    shape = list(blocks.shape[1:])
+    shape[dim] *= blocks.shape[0]
+    return jnp.moveaxis(blocks, 0, dim).reshape(shape)
+
+
+def collect(array, axis, dim):
+    size = lax.axis_size(axis)
+    right = [(i, (i + 1) % size) for i in range(size)]
+    tiles = [array]
+    while len(tiles) < size:
+        tiles.append(lax.ppermute(tiles[-1], axis, right))
+    index = lax.axis_index(axis)
+    tiles = jnp.stack(tiles)[(index - jnp.arange(size)) % size]
+    return laid_out(tiles, dim)
 
 
 def per_device(tile_list, tile_values, block_order, basis):
@@ -28,7 +45,7 @@
         present, owner_second // cols_count * own_blocks + second_slot % own_blocks, col_group
     )
     column_side = lax.all_gather(basis, "row", axis=0, tiled=True)
-    row_side = lax.all_gather(basis, "col", axis=0, tiled=True)
+    row_side = collect(basis, "col", 0)
     empty_block = jnp.zeros((1, edge, rank), basis.dtype)
     column_padded = jnp.concatenate([column_side, empty_block], axis=0)
     row_padded = jnp.concatenate([row_side, empty_block], axis=0)

time: 737 us -> 762 us (1.034)
  local copies, waits for them, and re-layouts: 58.5 us -> 71.2 us
  waiting for transfers between devices: 455 us -> 464 us
    ppermute x0 -> x7, waiting for transfers between devices: none -> 87.5 us  [collect(): tiles.append(lax.ppermute(tiles[-1], axis, right))]
    all_gather x1 -> x0, waiting for transfers between devices: 74 us -> none  [per_device(): row_side = lax.all_gather(basis, 'col', axis=0, tiled=True)]
  transfers between devices with their start and end apart: 6 -> 12, of which waited for: 4 -> 10; matrix products, arithmetic and copies ran while one was open for 15% -> 16% of each run, Pallas kernels for 0% -> 0%
where the time goes in v1:
time: 762 us; the launch traced here: 754 us
  waiting for transfers between devices  464 us (61%)
  other arithmetic  152 us (20%)
  local copies, waits for them, and re-layouts  71.2 us (9%)
  matrix products  33 us (4%)
  between operations  17 us (2%)
  starting transfers between devices  16 us (2%)
    psum x1, waiting for transfers between devices, per_device(): second = lax.psum(second_term, ('row', 'col'))  129 us
    psum x1, waiting for transfers between devices, per_device(): gram = lax.psum(gram_term, ('row', 'col'))  127 us
    reduce_scatter x1, waiting for transfers between devices, per_device(): lax.psum_scatter(row_partial, 'col', scatter_dimension=0, tiled=True)  122 us
    ppermute x7, waiting for transfers between devices, collect(): tiles.append(lax.ppermute(tiles[-1], axis, right))  87.5 us
    another operation x7, other arithmetic, per_device(): second_factor = jnp.linalg.cholesky(second)  34.8 us
    another operation x6, other arithmetic, per_device(): first_factor = jnp.linalg.cholesky(gram)  34 us
    another operation x3, other arithmetic, per_device(): lax.linalg.triangular_solve(first_factor, product, left_side=False, lower...  20 us
    another operation x2, other arithmetic, per_device(): lax.linalg.triangular_solve(second_factor, first_basis, left_side=False,...  19.7 us
  transfers between devices with their start and end apart: 12, of which 10 were waited for; matrix products, arithmetic and copies ran while one was open for 16% of the time, Pallas kernels for 0%

profile of v1, /device:TPU:0, one launch (start us, length us, event | category | flops | bytes accessed | tf_op | source)
XLA Modules:
  0.0 753.6 jit_solution(15524739183040842581)
XLA Ops:
  7.2 3.0 collective-permute-start
  10.3 15.2 %collective-permute-done = bf16[2,512,256]{2,1,0:T(8,128)(2,1)S(1)} collective-permute-done((bf16[2,512,256]{2,1,0:T(8,128)(2,1)}, bf16[2,512,256]{2,1,0:T(8,128)(2,1)S(1)}, u32[]{:S(2)}, u32[]{:S(2)}) %collective-permute-start) | collective-permute-done | bytes 524320 | tf_op jit(solution)/shard_map/ppermute | solution.py:18
  25.4 15.8 %collective-permute-done.1 = bf16[2,512,256]{2,1,0:T(8,128)(2,1)S(1)} collective-permute-done((bf16[2,512,256]{2,1,0:T(8,128)(2,1)S(1)}, bf16[2,512,256]{2,1,0:T(8,128)(2,1)S(1)}, u32[]{:S(2)}, u32[]{:S(2)}) %collective-permute-start.1) | collective-permute-done | bytes 524320 | tf_op jit(solution)/shard_map/ppermute | solution.py:18
  42.0 14.2 %collective-permute-done.2 = bf16[2,512,256]{2,1,0:T(8,128)(2,1)S(1)} collective-permute-done((bf16[2,512,256]{2,1,0:T(8,128)(2,1)S(1)}, bf16[2,512,256]{2,1,0:T(8,128)(2,1)S(1)}, u32[]{:S(2)}, u32[]{:S(2)}) %collective-permute-start.2) | collective-permute-done | bytes 524320 | tf_op jit(solution)/shard_map/ppermute | solution.py:18
  56.8 0.8 select_reduce_fusion.2
  58.4 11.8 %collective-permute-done.3 = bf16[2,512,256]{2,1,0:T(8,128)(2,1)S(1)} collective-permute-done((bf16[2,512,256]{2,1,0:T(8,128)(2,1)S(1)}, bf16[2,512,256]{2,1,0:T(8,128)(2,1)S(1)}, u32[]{:S(2)}, u32[]{:S(2)}) %collective-permute-start.3) | collective-permute-done | bytes 524320 | tf_op jit(solution)/shard_map/ppermute | solution.py:18
  70.3 1.9 bitcast_dynamic-update-slice_fusion.9
  72.1 11.3 %collective-permute-done.4 = bf16[2,512,256]{2,1,0:T(8,128)(2,1)S(1)} collective-permute-done((bf16[2,512,256]{2,1,0:T(8,128)(2,1)S(1)}, bf16[2,512,256]{2,1,0:T(8,128)(2,1)S(1)}, u32[]{:S(2)}, u32[]{:S(2)}) %collective-permute-start.4) | collective-permute-done | bytes 524320 | tf_op jit(solution)/shard_map/ppermute | solution.py:18
  83.4 0.8 bitcast_dynamic-update-slice_fusion.8
  84.3 0.9 bitcast_dynamic-update-slice_fusion.7
  85.1 0.8 bitcast_dynamic-update-slice_fusion.6
  86.0 9.8 %collective-permute-done.5 = bf16[2,512,256]{2,1,0:T(8,128)(2,1)S(1)} collective-permute-done((bf16[2,512,256]{2,1,0:T(8,128)(2,1)S(1)}, bf16[2,512,256]{2,1,0:T(8,128)(2,1)S(1)}, u32[]{:S(2)}, u32[]{:S(2)}) %collective-permute-start.5) | collective-permute-done | bytes 524320 | tf_op jit(solution)/shard_map/ppermute | solution.py:18
  95.8 0.8 bitcast_dynamic-update-slice_fusion.5
  96.6 0.8 bitcast_dynamic-update-slice_fusion.4
  97.5 0.8 bitcast_dynamic-update-slice_fusion.3
  98.3 9.4 %collective-permute-done.6 = bf16[2,512,256]{2,1,0:T(8,128)(2,1)S(1)} collective-permute-done((bf16[2,512,256]{2,1,0:T(8,128)(2,1)S(1)}, bf16[2,512,256]{2,1,0:T(8,128)(2,1)S(1)}, u32[]{:S(2)}, u32[]{:S(2)}) %collective-permute-start.6) | collective-permute-done | bytes 524320 | tf_op jit(solution)/shard_map/ppermute | solution.py:18
  107.7 0.8 bitcast_dynamic-update-slice_fusion.2
  108.5 5.0 gather_fusion.1
  113.5 4.6 concatenate.13
  118.1 5.0 gather_fusion.2
  123.1 10.2 %convolution_bitcast_fusion = f32[16,512,256]{1,2,0:T(8,128)} fusion(bf16[16,512,256]{2,1,0:T(8,128)(2,1)} %gather_fusion.2, bf16[16,512,512]{2,1,0:T(8,128)(2,1)} %param.8), kind=kOutput, calls=%fused_computation.17 | convolution fusion | flops 2147483648 | bytes 20971520 | tf_op jit(solution)/shard_map/tba,tbk->tak/dot_general | solution.py:57
  133.4 9.3 %copy.54 = f32[16,512,256]{2,1,0:T(8,128)} copy(f32[16,512,256]{1,2,0:T(8,128)} %convolution_bitcast_fusion) | data formatting | bytes 16777216 | tf_op jit(solution)/shard_map/tba,tbk->tak/dot_general | solution.py:57
  142.7 2.3 broadcast_in_dim.55
  144.9 15.6 %scatter_fusion.1 = f32[8,512,256]{2,1,0:T(8,128)} fusion(f32[8,512,256]{2,1,0:T(8,128)} %broadcast_in_dim.55, s32[16]{0:T(128)S(1)} %get-tuple-element.48, f32[16,512,256]{2,1,0:T(8,128)} %copy.54), kind=kCustom, calls=%fused_computation.4 | custom fusion | flops 2097152 | bytes 25165888 | tf_op jit(solution)/shard_map/scatter-add | solution.py:61
  160.7 1.7 concatenate.12
  162.4 2.7 gather_fusion
  165.2 11.7 %convolution_bitcast_fusion.1 = f32[16,512,256]{1,2,0:T(8,128)} fusion(bf16[16,512,256]{2,1,0:T(8,128)(2,1)} %gather_fusion, bf16[16,512,512]{2,1,0:T(8,128)(2,1)} %param.8), kind=kOutput, calls=%fused_computation.18 | convolution fusion | flops 2147483648 | bytes 20971520 | tf_op jit(solution)/shard_map/tab,tbk->tak/dot_general | solution.py:54
  176.9 9.5 %copy.52 = f32[16,512,256]{2,1,0:T(8,128)} copy(f32[16,512,256]{1,2,0:T(8,128)} %convolution_bitcast_fusion.1) | data formatting | bytes 16777216 | tf_op jit(solution)/shard_map/tab,tbk->tak/dot_general | solution.py:54
  186.4 4.1 broadcast_in_dim.48
  190.5 16.0 %scatter_fusion = f32[16,512,256]{2,1,0:T(8,128)} fusion(f32[16,512,256]{2,1,0:T(8,128)} %broadcast_in_dim.48, s32[16]{0:T(128)S(1)} %fusion.39, f32[16,512,256]{2,1,0:T(8,128)} %copy.52), kind=kCustom, calls=%fused_computation.3 | custom fusion | flops 2097152 | bytes 25165888 | tf_op jit(solution)/shard_map/scatter-add | solution.py:64
  206.5 12.8 %all-reduce.7.cloned.1.call-start = ((), (), s32[]{:S(2)}) async-start(), calls=%async_computation.5 | async-start | bytes 524288 | tf_op jit(solution)/shard_map/psum | solution.py:78
  219.3 5.4 copy.61
  224.7 2.6 convert_element_type.19
  227.3 0.9 copy-done
  229.0 1.0 subtract_convert_fusion
  230.6 1.8 fusion.7
  232.6 121.6 %reduce-scatter.3.cloned.1.call-done = f32[2,512,256]{2,1,0:T(8,128)} async-done(((f32[16,512,256]{2,1,0:T(8,128)}), f32[2,512,256]{2,1,0:T(8,128)}) %reduce-scatter.3.cloned.1.call-update) | async-done | bytes 1048592 | tf_op jit(solution)/shard_map/reduce_scatter | solution.py:66
  354.1 1.7 add.113
  355.8 2.5 convolution_bitcast_fusion.2
  358.4 0.8 fusion.17
  359.2 126.7 %all-reduce.7.cloned.1.call-done = f32[256,256]{0,1:T(8,128)} async-done(((f32[256,256]{0,1:T(8,128)}), f32[256,256]{0,1:T(8,128)}) %all-reduce.7.cloned.1.call-update) | async-done | bytes 262160 | tf_op jit(solution)/shard_map/psum | solution.py:78
  485.9 1.1 copy.57
  486.9 1.0 fusion.19
  487.9 11.7 %cholesky.130 = f32[128,128]{1,0:T(8,128)S(1)} custom-call(f32[128,128]{1,0:T(8,128)S(1)} %cholesky.194), custom_call_target="Cholesky" | custom-call | tf_op jit(solution)/shard_map/jit(cholesky)/cholesky | solution.py:79
  499.7 9.8 %custom-call.13 = f32[1,128,128]{1,2,0:T(8,128)S(1)} custom-call(f32[1,128,128]{2,1,0:T(8,128)S(1)} %get-tuple-element.61), custom_call_target="InvertDiagBlocksLowerTriangular" | custom-call | tf_op jit(solution)/shard_map/jit(cholesky)/cholesky | solution.py:79
  510.0 11.7 %cholesky.147 = f32[128,128]{1,0:T(8,128)S(1)} custom-call(f32[128,128]{1,0:T(8,128)S(1)} %convolution_subtract_fusion.3), custom_call_target="Cholesky" | custom-call | tf_op jit(solution)/shard_map/jit(cholesky)/cholesky | solution.py:79
  524.0 4.1 while.4
  524.6 1.4 bitcast_dynamic-update-slice_fusion.12
  526.6 1.4 bitcast_dynamic-update-slice_fusion.12
  528.1 20.0 %custom-call.14 = f32[2,128,128]{1,2,0:T(8,128)S(1)} custom-call(f32[2,128,128]{2,1,0:T(8,128)S(1)} %get-tuple-element.18), custom_call_target="InvertDiagBlocksLowerTriangular" | custom-call | tf_op jit(solution)/shard_map/triangular_solve/custom-call.0 | solution.py:80
  548.7 1.0 convolution_subtract_fusion.1
  550.3 1.7 fusion.10
  552.1 128.5 %all-reduce.9.cloned.1.call-done = (f32[256,256]{0,1:T(8,128)}, f32[256,256]{0,1:T(8,128)}) async-done(((f32[256,256]{0,1:T(8,128)}, f32[256,256]{0,1:T(8,128)}), (f32[256,256]{0,1:T(8,128)}, f32[256,256]{0,1:T(8,128)})) %all-reduce.9.cloned.1.call-update) | async-done | bytes 524304 | tf_op jit(solution)/shard_map/psum | solution.py:84
  680.6 1.1 copy.59
  681.7 1.0 fusion.18
  682.7 11.7 %cholesky.164 = f32[128,128]{1,0:T(8,128)S(1)} custom-call(f32[128,128]{1,0:T(8,128)S(1)} %cholesky.197), custom_call_target="Cholesky" | custom-call | tf_op jit(solution)/shard_map/jit(cholesky)/cholesky | solution.py:85
  694.5 9.8 %custom-call.15 = f32[1,128,128]{1,2,0:T(8,128)S(1)} custom-call(f32[1,128,128]{2,1,0:T(8,128)S(1)} %get-tuple-element.57), custom_call_target="InvertDiagBlocksLowerTriangular" | custom-call | tf_op jit(solution)/shard_map/jit(cholesky)/cholesky | solution.py:85
  704.8 11.9 %cholesky.181 = f32[128,128]{1,0:T(8,128)S(1)} custom-call(f32[128,128]{1,0:T(8,128)S(1)} %convolution_subtract_fusion.2), custom_call_target="Cholesky" | custom-call | tf_op jit(solution)/shard_map/jit(cholesky)/cholesky | solution.py:85
  719.4 4.0 while.5
  720.0 1.4 bitcast_dynamic-update-slice_fusion.13
  722.0 1.4 bitcast_dynamic-update-slice_fusion.13
  723.4 19.7 %custom-call.16 = f32[2,128,128]{1,2,0:T(8,128)S(1)} custom-call(f32[2,128,128]{2,1,0:T(8,128)S(1)} %get-tuple-element.19), custom_call_target="InvertDiagBlocksLowerTriangular" | custom-call | tf_op jit(solution)/shard_map/triangular_solve/custom-call.0 | solution.py:86
  745.0 1.0 copy.73
  746.0 0.8 copy.65
  (69 shorter events, 12.9 us)
Async XLA Ops:
  7.2 153.5 %all-gather.2.cloned.1.call-start = ((), (), s32[]{:S(2)}) async-start(), calls=%async_computation.2 | async-start | bytes 2621440 | tf_op jit(solution)/shard_map/all_gather | solution.py:47
  7.2 18.2 %collective-permute-start = (bf16[2,512,256]{2,1,0:T(8,128)(2,1)}, bf16[2,512,256]{2,1,0:T(8,128)(2,1)S(1)}, u32[]{:S(2)}, u32[]{:S(2)}) collective-permute-start(bf16[2,512,256]{2,1,0:T(8,128)(2,1)} %param.10), channel_id=1, source_target_pairs={{0,1},{1,2},{2,3},{3,4},{4,5},{5,6},{6,7},{7,0},{8,9},{9,10},{10,1... | collective-permute-start | bytes 1572872 | tf_op jit(solution)/shard_map/ppermute | solution.py:18
  25.4 15.8 %collective-permute-start.1 = (bf16[2,512,256]{2,1,0:T(8,128)(2,1)S(1)}, bf16[2,512,256]{2,1,0:T(8,128)(2,1)S(1)}, u32[]{:S(2)}, u32[]{:S(2)}) collective-permute-start(bf16[2,512,256]{2,1,0:T(8,128)(2,1)S(1)} %collective-permute-done), channel_id=1, source_target_pairs={{0,1},{1,2},{2,3},{3,4},{4,5},{5,6},{6,7},{7,0},{8,9},{9,10},{10,1... | collective-permute-start | bytes 1572872 | tf_op jit(solution)/shard_map/ppermute | solution.py:18
  41.2 14.9 %collective-permute-start.2 = (bf16[2,512,256]{2,1,0:T(8,128)(2,1)S(1)}, bf16[2,512,256]{2,1,0:T(8,128)(2,1)S(1)}, u32[]{:S(2)}, u32[]{:S(2)}) collective-permute-start(bf16[2,512,256]{2,1,0:T(8,128)(2,1)S(1)} %collective-permute-done.1), channel_id=1, source_target_pairs={{0,1},{1,2},{2,3},{3,4},{4,5},{5,6},{6,7},{7,0},{8,9},{9,10},{10,1... | collective-permute-start | bytes 1572872 | tf_op jit(solution)/shard_map/ppermute | solution.py:18
  41.2 191.3 %reduce-scatter.5.cloned.1.call-start = ((), (), s32[]{:S(2)}) async-start(), calls=%async_computation.4 | async-start | bytes 5242880 | tf_op jit(solution)/shard_map/reduce_scatter | solution.py:75
  56.1 14.1 %collective-permute-start.3 = (bf16[2,512,256]{2,1,0:T(8,128)(2,1)S(1)}, bf16[2,512,256]{2,1,0:T(8,128)(2,1)S(1)}, u32[]{:S(2)}, u32[]{:S(2)}) collective-permute-start(bf16[2,512,256]{2,1,0:T(8,128)(2,1)S(1)} %collective-permute-done.2), channel_id=1, source_target_pairs={{0,1},{1,2},{2,3},{3,4},{4,5},{5,6},{6,7},{7,0},{8,9},{9,10},{10,1... | collective-permute-start | bytes 1572872 | tf_op jit(solution)/shard_map/ppermute | solution.py:18
  70.2 13.2 %collective-permute-start.4 = (bf16[2,512,256]{2,1,0:T(8,128)(2,1)S(1)}, bf16[2,512,256]{2,1,0:T(8,128)(2,1)S(1)}, u32[]{:S(2)}, u32[]{:S(2)}) collective-permute-start(bf16[2,512,256]{2,1,0:T(8,128)(2,1)S(1)} %collective-permute-done.3), channel_id=1, source_target_pairs={{0,1},{1,2},{2,3},{3,4},{4,5},{5,6},{6,7},{7,0},{8,9},{9,10},{10,1... | collective-permute-start | bytes 1572872 | tf_op jit(solution)/shard_map/ppermute | solution.py:18
  83.4 12.4 %collective-permute-start.5 = (bf16[2,512,256]{2,1,0:T(8,128)(2,1)S(1)}, bf16[2,512,256]{2,1,0:T(8,128)(2,1)S(1)}, u32[]{:S(2)}, u32[]{:S(2)}) collective-permute-start(bf16[2,512,256]{2,1,0:T(8,128)(2,1)S(1)} %collective-permute-done.4), channel_id=1, source_target_pairs={{0,1},{1,2},{2,3},{3,4},{4,5},{5,6},{6,7},{7,0},{8,9},{9,10},{10,1... | collective-permute-start | bytes 1572872 | tf_op jit(solution)/shard_map/ppermute | solution.py:18
  95.8 11.9 %collective-permute-start.6 = (bf16[2,512,256]{2,1,0:T(8,128)(2,1)S(1)}, bf16[2,512,256]{2,1,0:T(8,128)(2,1)S(1)}, u32[]{:S(2)}, u32[]{:S(2)}) collective-permute-start(bf16[2,512,256]{2,1,0:T(8,128)(2,1)S(1)} %collective-permute-done.5), channel_id=1, source_target_pairs={{0,1},{1,2},{2,3},{3,4},{4,5},{5,6},{6,7},{7,0},{8,9},{9,10},{10,1... | collective-permute-start | bytes 1572872 | tf_op jit(solution)/shard_map/ppermute | solution.py:18
  160.6 193.6 %reduce-scatter.3.cloned.1.call-start = ((), (), s32[]{:S(2)}) async-start(), calls=%async_computation.3 | async-start | bytes 9437184 | tf_op jit(solution)/shard_map/reduce_scatter | solution.py:66
  206.5 279.3 %all-reduce.7.cloned.1.call-start = ((), (), s32[]{:S(2)}) async-start(), calls=%async_computation.5 | async-start | bytes 524288 | tf_op jit(solution)/shard_map/psum | solution.py:78
  224.7 3.5 copy-start
  229.0 1.6 copy-start.1
  358.4 322.3 %all-reduce.9.cloned.1.call-start = ((), (), s32[]{:S(2)}) async-start(), calls=%async_computation.6 | async-start | bytes 1048576 | tf_op jit(solution)/shard_map/psum | solution.py:84
  704.5 41.5 %copy-start.2 = (f32[256,256]{0,1:T(8,128)S(1)}, f32[256,256]{0,1:T(8,128)}, u32[]{:S(2)}) copy-start(f32[256,256]{0,1:T(8,128)} %get-tuple-element.45) | copy-start | bytes 786436
Sparse Core Ops, SparseCore 0:
  41.4 23.7 all-gather.1
  160.7 42.2 reduce-scatter.4
  206.6 147.4 reduce-scatter.2
  360.1 125.7 all-reduce.6
  552.2 128.3 all-reduce.8
